TPU v7x, 32 devices: a whole 2x2x4 slice. The times are simulated.
32 devices in a mesh: grp: 2 (over y), row: 4 (over z), col: 2 (over x), sub: 2 (over core).
Axes of the slice: x: 2, y: 2, z: 4, core: 2. Of those that a mesh axis runs over, the one named last changes fastest.
Arguments:
- left_features: bfloat16 [256, 256, 128], P(('grp', 'row'), ('col', 'sub')), parts along dimension 0, may hold values from -16 to 16
- right_features: bfloat16 [256, 256, 128], P(('grp', 'row'), ('col', 'sub')), parts along dimension 0, may hold values from -16 to 16
- left_image: float32 [3, 256, 256], P(None, ('grp', 'row'), ('col', 'sub')), parts along dimension 1, may hold values from -4 to 4
- query_key: bfloat16 [128, 128], replicated, may hold values from -0.5 to 0.5
- value_weight: bfloat16 [128, 128], replicated, may hold values from -0.5 to 0.5
- out_weight: bfloat16 [128, 128], replicated, may hold values from -0.5 to 0.5
- occlusion_weight: float32 [128], replicated, may hold values from -0.5 to 0.5
- first_conv: bfloat16 [9, 64, 5], replicated, may hold values from -0.875 to 0.875
- middle_conv: bfloat16 [3, 9, 64, 64], replicated, may hold values from -0.25 to 0.25
- last_conv: bfloat16 [9, 2, 64], replicated, may hold values from -0.25 to 0.25
Outputs:
- disparity_out: float32 [256, 256], P(('grp', 'row'), ('col', 'sub')), parts along dimension 0
- occlusion_out: float32 [256, 256], P(('grp', 'row'), ('col', 'sub')), parts along dimension 0
There are 2 independent parts, one for each index of `grp`. A program takes and returns all parts, laid end to end along the dimension named above; an argument that names none is the same for every part. Nothing has to cross between parts.
All inputs are finite; a program needn't handle non-finite values.
Results may differ from a plain program's by a relative error of at most 0.0033.
Values may be sent and summed in bfloat16 or wider, within the bound.
No kernel may reach another device: no remote copies, remote signals or barrier semaphores. Data moves between devices by JAX's collectives and lax.ppermute only.
A program may use at most 64 MiB of HBM per device.

v0:
```python
import jax
import jax.numpy as jnp
from jax import lax
from jax.sharding import PartitionSpec as P

C = 128
HEADS = 8
HEAD = 16


def with_halo(cells, sides, width):
    for axis, dim in sides:
        count = lax.axis_size(axis)
        ends = count - 1
        head = lax.slice_in_dim(cells, 0, width, axis=dim)
        tail = lax.slice_in_dim(cells, cells.shape[dim] - width, cells.shape[dim], axis=dim)
        cells = jnp.concatenate(
            [
                lax.ppermute(tail, axis, [(i, (i + 1) % count) for i in range(ends)]),
                cells,
                lax.ppermute(head, axis, [((i + 1) % count, i) for i in range(ends)]),
            ],
            axis=dim,
        )
    return cells


def conv_valid(source, weight):
    height = source.shape[1] - 2
    across = source.shape[2] - 2
    summed = jnp.zeros((weight.shape[1], height, across), jnp.float32)
    for offset in range(9):
        window = source[:, offset // 3 : offset // 3 + height, offset % 3 : offset % 3 + across]
        summed = summed + jnp.einsum(
            "oc,crw->orw", weight[offset], window, preferred_element_type=jnp.float32
        )
    return summed


def layer_same(source, weight):
    padded = with_halo(source, (("row", 1), (("col", "sub"), 2)), 1)
    return conv_valid(padded, weight)


def occlusion_logit(gathered, out_weight, occlusion_weight):
    attended = jnp.einsum("rwc,cd->rwd", gathered, out_weight, preferred_element_type=jnp.float32)
    centre = jnp.mean(attended, axis=-1, keepdims=True)
    spread = jnp.mean((attended - centre) ** 2, axis=-1, keepdims=True)
    normalized = (attended - centre) * lax.rsqrt(spread + 1e-05)
    return jnp.einsum("rwc,c->rw", normalized, occlusion_weight, precision=lax.Precision.HIGHEST)


def per_device(
    left_features,
    right_features,
    left_image,
    query_key,
    value_weight,
    out_weight,
    occlusion_weight,
    first_conv,
    middle_conv,
    last_conv,
):
    tile_rows = left_features.shape[0]
    tile_cols = left_features.shape[1]
    group_size = lax.axis_size(("col", "sub"))
    row_length = tile_cols * group_size
    scaling = HEAD ** (-0.5)
    positions = jnp.arange(row_length)
    allowed = positions[None, :] <= positions[:, None]
    places = positions.astype(jnp.float32)

    def attend(inputs):
        query_block, key_block, value_block = inputs
        scores = jnp.einsum(
            "bihd,bjhd->bhij", query_block, key_block, preferred_element_type=jnp.float32
        )
        scores = jnp.where(allowed[None, None], scores, -jnp.inf)
        largest = jnp.max(scores, axis=-1, keepdims=True)
        exponent = jnp.exp(scores - largest)
        totals = jnp.sum(exponent, axis=-1, keepdims=True)
        probabilities = (exponent / totals).astype(jnp.bfloat16)
        blended = jnp.einsum(
            "bhij,bjhd->bihd", probabilities, value_block, preferred_element_type=jnp.float32
        ).astype(jnp.bfloat16)
        weighted = jnp.einsum("bhij,j->bhi", exponent, places, precision=lax.Precision.HIGHEST)
        shifts = places[None, None, :] - weighted / totals[..., 0]
        return (blended, jnp.sum(shifts, axis=1))

    band_count = tile_rows // group_size
    full_left, full_right = (
        lax.all_to_all(left_features, ("col", "sub"), split_axis=0, concat_axis=1, tiled=True),
        lax.all_to_all(right_features, ("col", "sub"), split_axis=0, concat_axis=1, tiled=True),
    )
    queries = (
        jnp.einsum("rwc,cd->rwd", full_left, query_key, preferred_element_type=jnp.float32)
        * scaling
    ).astype(jnp.bfloat16)
    keys = jnp.einsum(
        "rwc,cd->rwd", full_right, query_key, preferred_element_type=jnp.float32
    ).astype(jnp.bfloat16)
    values = jnp.einsum(
        "rwc,cd->rwd", full_right, value_weight, preferred_element_type=jnp.float32
    ).astype(jnp.bfloat16)
    block_shape = (band_count, 1, row_length, HEADS, HEAD)
    blended, shift_sums = lax.map(
        attend,
        (queries.reshape(block_shape), keys.reshape(block_shape), values.reshape(block_shape)),
    )
    head_out = blended.reshape(band_count, row_length, C)
    band_disparity = shift_sums.reshape(band_count, row_length) * (8.0 / (HEADS * row_length))
    band_occlusion = occlusion_logit(head_out, out_weight, occlusion_weight)
    maps = lax.all_to_all(
        jnp.stack([band_disparity, band_occlusion]),
        ("col", "sub"),
        split_axis=2,
        concat_axis=1,
        tiled=True,
    )
    disparity = maps[0]
    occlusion = maps[1]
    stacked = jnp.concatenate([disparity[None], occlusion[None], left_image], axis=0).astype(
        jnp.bfloat16
    )
    layer_one = jax.nn.relu(layer_same(stacked, first_conv)).astype(jnp.bfloat16)
    layer_two = jax.nn.relu(layer_same(layer_one, middle_conv[0])).astype(jnp.bfloat16)
    layer_three = jax.nn.relu(
        layer_one.astype(jnp.float32) + layer_same(layer_two, middle_conv[1])
    ).astype(jnp.bfloat16)
    layer_four = jax.nn.relu(layer_same(layer_three, middle_conv[2])).astype(jnp.bfloat16)
    correction = layer_same(layer_four, last_conv)
    disparity_out = disparity + correction[0]
    occlusion_out = jax.nn.sigmoid(occlusion + correction[1])
    return (disparity_out, occlusion_out)


def solution(mesh):
    placed = (
        P(("grp", "row"), ("col", "sub"), None),
        P(("grp", "row"), ("col", "sub"), None),
        P(None, ("grp", "row"), ("col", "sub")),
        P(),
        P(),
        P(),
        P(),
        P(),
        P(),
        P(),
    )
    return jax.shard_map(
        per_device,
        mesh=mesh,
        in_specs=placed,
        out_specs=(P(("grp", "row"), ("col", "sub")), P(("grp", "row"), ("col", "sub"))),
        check_vma=False,
    )
```

profile of v0, /device:TPU:1, one launch (start us, length us, event | category | flops | bytes accessed | tf_op | source)
XLA Modules:
  0.0 168.5 jit_solution(7081243207091826723)
XLA Ops:
  0.6 4.3 %all-to-all-start = ((bf16[32,64,128]{2,1,0:T(8,128)(2,1)}), bf16[32,64,128]{2,1,0:T(8,128)(2,1)S(1)}, u32[]{:S(2)}, u32[]{:S(2)}) async-start(bf16[32,64,128]{2,1,0:T(8,128)(2,1)} %param.13), calls=%async_computation | async-start | bytes 1048576 | tf_op jit(solution)/shard_map/all_to_all | solution.py:94
  4.9 7.8 %all-to-all-done = bf16[32,64,128]{2,1,0:T(8,128)(2,1)S(1)} async-done(((bf16[32,64,128]{2,1,0:T(8,128)(2,1)}), bf16[32,64,128]{2,1,0:T(8,128)(2,1)S(1)}, u32[]{:S(2)}, u32[]{:S(2)}) %all-to-all-start) | async-done | bytes 524320 | tf_op jit(solution)/shard_map/all_to_all | solution.py:94
  12.7 4.5 %all-to-all-start.1 = ((bf16[32,64,128]{2,1,0:T(8,128)(2,1)}), bf16[32,64,128]{2,1,0:T(8,128)(2,1)S(1)}, u32[]{:S(2)}, u32[]{:S(2)}) async-start(bf16[32,64,128]{2,1,0:T(8,128)(2,1)} %param.12), calls=%async_computation.1 | async-start | bytes 1048576 | tf_op jit(solution)/shard_map/all_to_all | solution.py:93
  19.1 6.1 %all-to-all-done.1 = bf16[32,64,128]{2,1,0:T(8,128)(2,1)S(1)} async-done(((bf16[32,64,128]{2,1,0:T(8,128)(2,1)}), bf16[32,64,128]{2,1,0:T(8,128)(2,1)S(1)}, u32[]{:S(2)}, u32[]{:S(2)}) %all-to-all-start.1) | async-done | bytes 524320 | tf_op jit(solution)/shard_map/all_to_all | solution.py:93
  25.6 36.1 %while.14 = (s32[]{:T(128)}, bf16[8,1,256,8,16]{2,4,3,1,0:T(8,128)(2,1)}, f32[8,1,256]{2,0,1:T(8,128)S(1)}, bf16[8,1,256,8,16]{2,4,3,1,0:T(8,128)(2,1)}, bf16[8,...) while((s32[]{:T(128)}, ...), condition=%wide.region_4.5_spmd.clone.clone, body=%wide.region_0.4_spmd.clone.clone.sunk | while | flops 45713408 | bytes 9060441 | solution.py:107
  65.2 4.1 %all-to-all-start.2 = ((f32[4,1,1024]{2,1,0:T(1,128)}), f32[4,1,1024]{2,1,0:T(1,128)S(1)}, u32[]{:S(2)}, u32[]{:S(2)}) async-start(f32[4,1,1024]{2,1,0:T(1,128)} %reshape.211), calls=%async_computation.2 | async-start | bytes 32768 | tf_op jit(solution)/shard_map/all_to_all | solution.py:114
  69.3 3.1 %all-to-all-done.2 = f32[4,1,1024]{2,1,0:T(1,128)S(1)} async-done(((f32[4,1,1024]{2,1,0:T(1,128)}), f32[4,1,1024]{2,1,0:T(1,128)S(1)}, u32[]{:S(2)}, u32[]{:S(2)}) %all-to-all-start.2) | async-done | bytes 16416 | tf_op jit(solution)/shard_map/all_to_all | solution.py:114
  74.2 3.9 %collective-permute-start = (bf16[5,1,64]{2,1,0:T(2,128)(2,1)S(1)}, bf16[5,1,64]{2,1,0:T(2,128)(2,1)S(1)}, u32[]{:S(2)}, u32[]{:S(2)}) collective-permute-start(bf16[5,1,64]{2,1,0:T(2,128)(2,1)S(1)} %get-tuple-element.177), channel_id=1, source_target_pairs={{0,4},{4,8},{8,12},{1,5},{5,9},{9,13},{2,6},{6,10},{10,14},{3,7},{... | collective-permute-start | bytes 1928 | tf_op jit(solution)/shard_map/ppermute | solution.py:19
  79.4 3.0 %collective-permute-done.1 = bf16[5,1,64]{2,1,0:T(2,128)(2,1)S(1)} collective-permute-done((bf16[5,1,64]{2,1,0:T(2,128)(2,1)S(1)}, bf16[5,1,64]{2,1,0:T(2,128)(2,1)S(1)}, u32[]{:S(2)}, u32[]{:S(2)}) %collective-permute-start.1) | collective-permute-done | bytes 672 | tf_op jit(solution)/shard_map/ppermute | solution.py:21
  82.6 3.7 %collective-permute-start.2 = (bf16[5,34,1]{2,1,0:T(8,128)(2,1)S(1)}, bf16[5,34,1]{2,1,0:T(8,128)(2,1)S(1)}, u32[]{:S(2)}, u32[]{:S(2)}) collective-permute-start(bf16[5,34,1]{2,1,0:T(8,128)(2,1)S(1)} %get-tuple-element.171), channel_id=1, source_target_pairs={{0,1},{1,2},{2,3},{4,5},{5,6},{6,7},{8,9},{9,10},{10,11},{12,13},{... | collective-permute-start | bytes 1028 | tf_op jit(solution)/shard_map/ppermute | solution.py:19
  88.6 3.1 %collective-permute-done.3 = bf16[5,34,1]{2,1,0:T(8,128)(2,1)S(1)} collective-permute-done((bf16[5,34,1]{2,1,0:T(8,128)(2,1)S(1)}, bf16[5,34,1]{2,1,0:T(8,128)(2,1)S(1)}, u32[]{:S(2)}, u32[]{:S(2)}) %collective-permute-start.3) | collective-permute-done | bytes 372 | tf_op jit(solution)/shard_map/ppermute | solution.py:21
  94.8 3.2 %collective-permute-start.4 = (bf16[64,1,64]{0,2,1:T(8,128)(2,1)S(1)}, bf16[64,1,64]{0,2,1:T(8,128)(2,1)S(1)}, u32[]{:S(2)}, u32[]{:S(2)}) collective-permute-start(bf16[64,1,64]{0,2,1:T(8,128)(2,1)S(1)} %get-tuple-element.163), channel_id=1, source_target_pairs={{0,4},{4,8},{8,12},{1,5},{5,9},{9,13},{2,6},{6,10},{10,14},{3,7},{... | collective-permute-start | bytes 24584 | tf_op jit(solution)/shard_map/ppermute | solution.py:19
  99.7 2.9 %collective-permute-done.5 = bf16[64,1,64]{0,2,1:T(8,128)(2,1)S(1)} collective-permute-done((bf16[64,1,64]{0,2,1:T(8,128)(2,1)S(1)}, bf16[64,1,64]{0,2,1:T(8,128)(2,1)S(1)}, u32[]{:S(2)}, u32[]{:S(2)}) %collective-permute-start.5) | collective-permute-done | bytes 8224 | tf_op jit(solution)/shard_map/ppermute | solution.py:21
  102.6 3.3 %collective-permute-start.6 = (bf16[64,34,1]{0,2,1:T(2,128)(2,1)S(1)}, bf16[64,34,1]{0,2,1:T(2,128)(2,1)S(1)}, u32[]{:S(2)}, u32[]{:S(2)}) collective-permute-start(bf16[64,34,1]{0,2,1:T(2,128)(2,1)S(1)} %get-tuple-element.155), channel_id=1, source_target_pairs={{0,1},{1,2},{2,3},{4,5},{5,6},{6,7},{8,9},{9,10},{10,11},{12,13},{... | collective-permute-start | bytes 13064 | tf_op jit(solution)/shard_map/ppermute | solution.py:19
  108.4 2.5 %collective-permute-done.7 = bf16[64,34,1]{0,2,1:T(2,128)(2,1)S(1)} collective-permute-done((bf16[64,34,1]{0,2,1:T(2,128)(2,1)S(1)}, bf16[64,34,1]{0,2,1:T(2,128)(2,1)S(1)}, u32[]{:S(2)}, u32[]{:S(2)}) %collective-permute-start.7) | collective-permute-done | bytes 4384 | tf_op jit(solution)/shard_map/ppermute | solution.py:21
  113.3 3.4 %collective-permute-start.8 = (bf16[64,1,64]{0,2,1:T(8,128)(2,1)S(1)}, bf16[64,1,64]{0,2,1:T(8,128)(2,1)S(1)}, u32[]{:S(2)}, u32[]{:S(2)}) collective-permute-start(bf16[64,1,64]{0,2,1:T(8,128)(2,1)S(1)} %get-tuple-element.161), channel_id=1, source_target_pairs={{0,4},{4,8},{8,12},{1,5},{5,9},{9,13},{2,6},{6,10},{10,14},{3,7},{... | collective-permute-start | bytes 24584 | tf_op jit(solution)/shard_map/ppermute | solution.py:19
  118.3 2.9 %collective-permute-done.9 = bf16[64,1,64]{0,2,1:T(8,128)(2,1)S(1)} collective-permute-done((bf16[64,1,64]{0,2,1:T(8,128)(2,1)S(1)}, bf16[64,1,64]{0,2,1:T(8,128)(2,1)S(1)}, u32[]{:S(2)}, u32[]{:S(2)}) %collective-permute-start.9) | collective-permute-done | bytes 8224 | tf_op jit(solution)/shard_map/ppermute | solution.py:21
  121.3 3.4 %collective-permute-start.10 = (bf16[64,34,1]{0,2,1:T(2,128)(2,1)S(1)}, bf16[64,34,1]{0,2,1:T(2,128)(2,1)S(1)}, u32[]{:S(2)}, u32[]{:S(2)}) collective-permute-start(bf16[64,34,1]{0,2,1:T(2,128)(2,1)S(1)} %get-tuple-element.151), channel_id=1, source_target_pairs={{0,1},{1,2},{2,3},{4,5},{5,6},{6,7},{8,9},{9,10},{10,11},{12,13},{... | collective-permute-start | bytes 13064 | tf_op jit(solution)/shard_map/ppermute | solution.py:19
  127.2 2.5 %collective-permute-done.11 = bf16[64,34,1]{0,2,1:T(2,128)(2,1)S(1)} collective-permute-done((bf16[64,34,1]{0,2,1:T(2,128)(2,1)S(1)}, bf16[64,34,1]{0,2,1:T(2,128)(2,1)S(1)}, u32[]{:S(2)}, u32[]{:S(2)}) %collective-permute-start.11) | collective-permute-done | bytes 4384 | tf_op jit(solution)/shard_map/ppermute | solution.py:21
  135.4 2.9 %collective-permute-done.13 = bf16[64,1,64]{0,2,1:T(8,128)(2,1)S(1)} collective-permute-done((bf16[64,1,64]{0,2,1:T(8,128)(2,1)S(1)}, bf16[64,1,64]{0,2,1:T(8,128)(2,1)S(1)}, u32[]{:S(2)}, u32[]{:S(2)}) %collective-permute-start.13) | collective-permute-done | bytes 8224 | tf_op jit(solution)/shard_map/ppermute | solution.py:21
  138.4 3.4 %collective-permute-start.14 = (bf16[64,34,1]{0,2,1:T(2,128)(2,1)S(1)}, bf16[64,34,1]{0,2,1:T(2,128)(2,1)S(1)}, u32[]{:S(2)}, u32[]{:S(2)}) collective-permute-start(bf16[64,34,1]{0,2,1:T(2,128)(2,1)S(1)} %get-tuple-element.147), channel_id=1, source_target_pairs={{0,1},{1,2},{2,3},{4,5},{5,6},{6,7},{8,9},{9,10},{10,11},{12,13},{... | collective-permute-start | bytes 13064 | tf_op jit(solution)/shard_map/ppermute | solution.py:19
  144.3 2.5 %collective-permute-done.15 = bf16[64,34,1]{0,2,1:T(2,128)(2,1)S(1)} collective-permute-done((bf16[64,34,1]{0,2,1:T(2,128)(2,1)S(1)}, bf16[64,34,1]{0,2,1:T(2,128)(2,1)S(1)}, u32[]{:S(2)}, u32[]{:S(2)}) %collective-permute-start.15) | collective-permute-done | bytes 4384 | tf_op jit(solution)/shard_map/ppermute | solution.py:21
  152.6 2.7 %collective-permute-done.17 = bf16[64,1,64]{0,2,1:T(8,128)(2,1)S(1)} collective-permute-done((bf16[64,1,64]{0,2,1:T(8,128)(2,1)S(1)}, bf16[64,1,64]{0,2,1:T(8,128)(2,1)S(1)}, u32[]{:S(2)}, u32[]{:S(2)}) %collective-permute-start.17) | collective-permute-done | bytes 8224 | tf_op jit(solution)/shard_map/ppermute | solution.py:21
  155.4 3.4 %collective-permute-start.18 = (bf16[64,34,1]{0,2,1:T(2,128)(2,1)S(1)}, bf16[64,34,1]{0,2,1:T(2,128)(2,1)S(1)}, u32[]{:S(2)}, u32[]{:S(2)}) collective-permute-start(bf16[64,34,1]{0,2,1:T(2,128)(2,1)S(1)} %get-tuple-element.143), channel_id=1, source_target_pairs={{0,1},{1,2},{2,3},{4,5},{5,6},{6,7},{8,9},{9,10},{10,11},{12,13},{... | collective-permute-start | bytes 13064 | tf_op jit(solution)/shard_map/ppermute | solution.py:19
  (196 shorter events, 84.4 us)
Async XLA Ops:
  0.6 12.1 %all-to-all-start = ((bf16[32,64,128]{2,1,0:T(8,128)(2,1)}), bf16[32,64,128]{2,1,0:T(8,128)(2,1)S(1)}, u32[]{:S(2)}, u32[]{:S(2)}) async-start(bf16[32,64,128]{2,1,0:T(8,128)(2,1)} %param.13), calls=%async_computation | async-start | bytes 1048576 | tf_op jit(solution)/shard_map/all_to_all | solution.py:94
  12.7 12.5 %all-to-all-start.1 = ((bf16[32,64,128]{2,1,0:T(8,128)(2,1)}), bf16[32,64,128]{2,1,0:T(8,128)(2,1)S(1)}, u32[]{:S(2)}, u32[]{:S(2)}) async-start(bf16[32,64,128]{2,1,0:T(8,128)(2,1)} %param.12), calls=%async_computation.1 | async-start | bytes 1048576 | tf_op jit(solution)/shard_map/all_to_all | solution.py:93
  25.6 36.1 %copy-start.4 = (bf16[128,128]{1,0:T(8,128)(2,1)S(1)}, bf16[128,128]{1,0:T(8,128)(2,1)}, u32[]{:S(2)}) copy-start(bf16[128,128]{1,0:T(8,128)(2,1)} %param.17) | copy-start | bytes 98308
  65.2 7.2 %all-to-all-start.2 = ((f32[4,1,1024]{2,1,0:T(1,128)}), f32[4,1,1024]{2,1,0:T(1,128)S(1)}, u32[]{:S(2)}, u32[]{:S(2)}) async-start(f32[4,1,1024]{2,1,0:T(1,128)} %reshape.211), calls=%async_computation.2 | async-start | bytes 32768 | tf_op jit(solution)/shard_map/all_to_all | solution.py:114
  74.2 5.2 %collective-permute-start = (bf16[5,1,64]{2,1,0:T(2,128)(2,1)S(1)}, bf16[5,1,64]{2,1,0:T(2,128)(2,1)S(1)}, u32[]{:S(2)}, u32[]{:S(2)}) collective-permute-start(bf16[5,1,64]{2,1,0:T(2,128)(2,1)S(1)} %get-tuple-element.177), channel_id=1, source_target_pairs={{0,4},{4,8},{8,12},{1,5},{5,9},{9,13},{2,6},{6,10},{10,14},{3,7},{... | collective-permute-start | bytes 1928 | tf_op jit(solution)/shard_map/ppermute | solution.py:19
  78.1 4.3 %collective-permute-start.1 = (bf16[5,1,64]{2,1,0:T(2,128)(2,1)S(1)}, bf16[5,1,64]{2,1,0:T(2,128)(2,1)S(1)}, u32[]{:S(2)}, u32[]{:S(2)}) collective-permute-start(bf16[5,1,64]{2,1,0:T(2,128)(2,1)S(1)} %get-tuple-element.178), channel_id=1, source_target_pairs={{4,0},{8,4},{12,8},{5,1},{9,5},{13,9},{6,2},{10,6},{14,10},{7,3},{... | collective-permute-start | bytes 1928 | tf_op jit(solution)/shard_map/ppermute | solution.py:21
  82.6 6.0 %collective-permute-start.2 = (bf16[5,34,1]{2,1,0:T(8,128)(2,1)S(1)}, bf16[5,34,1]{2,1,0:T(8,128)(2,1)S(1)}, u32[]{:S(2)}, u32[]{:S(2)}) collective-permute-start(bf16[5,34,1]{2,1,0:T(8,128)(2,1)S(1)} %get-tuple-element.171), channel_id=1, source_target_pairs={{0,1},{1,2},{2,3},{4,5},{5,6},{6,7},{8,9},{9,10},{10,11},{12,13},{... | collective-permute-start | bytes 1028 | tf_op jit(solution)/shard_map/ppermute | solution.py:19
  86.3 5.4 %collective-permute-start.3 = (bf16[5,34,1]{2,1,0:T(8,128)(2,1)S(1)}, bf16[5,34,1]{2,1,0:T(8,128)(2,1)S(1)}, u32[]{:S(2)}, u32[]{:S(2)}) collective-permute-start(bf16[5,34,1]{2,1,0:T(8,128)(2,1)S(1)} %get-tuple-element.172), channel_id=1, source_target_pairs={{1,0},{2,1},{3,2},{5,4},{6,5},{7,6},{9,8},{10,9},{11,10},{13,12},{... | collective-permute-start | bytes 1028 | tf_op jit(solution)/shard_map/ppermute | solution.py:21
  94.8 4.8 %collective-permute-start.4 = (bf16[64,1,64]{0,2,1:T(8,128)(2,1)S(1)}, bf16[64,1,64]{0,2,1:T(8,128)(2,1)S(1)}, u32[]{:S(2)}, u32[]{:S(2)}) collective-permute-start(bf16[64,1,64]{0,2,1:T(8,128)(2,1)S(1)} %get-tuple-element.163), channel_id=1, source_target_pairs={{0,4},{4,8},{8,12},{1,5},{5,9},{9,13},{2,6},{6,10},{10,14},{3,7},{... | collective-permute-start | bytes 24584 | tf_op jit(solution)/shard_map/ppermute | solution.py:19
  98.0 4.5 %collective-permute-start.5 = (bf16[64,1,64]{0,2,1:T(8,128)(2,1)S(1)}, bf16[64,1,64]{0,2,1:T(8,128)(2,1)S(1)}, u32[]{:S(2)}, u32[]{:S(2)}) collective-permute-start(bf16[64,1,64]{0,2,1:T(8,128)(2,1)S(1)} %get-tuple-element.164), channel_id=1, source_target_pairs={{4,0},{8,4},{12,8},{5,1},{9,5},{13,9},{6,2},{10,6},{14,10},{7,3},{... | collective-permute-start | bytes 24584 | tf_op jit(solution)/shard_map/ppermute | solution.py:21
  102.6 5.9 %collective-permute-start.6 = (bf16[64,34,1]{0,2,1:T(2,128)(2,1)S(1)}, bf16[64,34,1]{0,2,1:T(2,128)(2,1)S(1)}, u32[]{:S(2)}, u32[]{:S(2)}) collective-permute-start(bf16[64,34,1]{0,2,1:T(2,128)(2,1)S(1)} %get-tuple-element.155), channel_id=1, source_target_pairs={{0,1},{1,2},{2,3},{4,5},{5,6},{6,7},{8,9},{9,10},{10,11},{12,13},{... | collective-permute-start | bytes 13064 | tf_op jit(solution)/shard_map/ppermute | solution.py:19
  105.9 5.1 %collective-permute-start.7 = (bf16[64,34,1]{0,2,1:T(2,128)(2,1)S(1)}, bf16[64,34,1]{0,2,1:T(2,128)(2,1)S(1)}, u32[]{:S(2)}, u32[]{:S(2)}) collective-permute-start(bf16[64,34,1]{0,2,1:T(2,128)(2,1)S(1)} %get-tuple-element.156), channel_id=1, source_target_pairs={{1,0},{2,1},{3,2},{5,4},{6,5},{7,6},{9,8},{10,9},{11,10},{13,12},{... | collective-permute-start | bytes 13064 | tf_op jit(solution)/shard_map/ppermute | solution.py:21
  113.3 5.0 %collective-permute-start.8 = (bf16[64,1,64]{0,2,1:T(8,128)(2,1)S(1)}, bf16[64,1,64]{0,2,1:T(8,128)(2,1)S(1)}, u32[]{:S(2)}, u32[]{:S(2)}) collective-permute-start(bf16[64,1,64]{0,2,1:T(8,128)(2,1)S(1)} %get-tuple-element.161), channel_id=1, source_target_pairs={{0,4},{4,8},{8,12},{1,5},{5,9},{9,13},{2,6},{6,10},{10,14},{3,7},{... | collective-permute-start | bytes 24584 | tf_op jit(solution)/shard_map/ppermute | solution.py:19
  116.7 4.5 %collective-permute-start.9 = (bf16[64,1,64]{0,2,1:T(8,128)(2,1)S(1)}, bf16[64,1,64]{0,2,1:T(8,128)(2,1)S(1)}, u32[]{:S(2)}, u32[]{:S(2)}) collective-permute-start(bf16[64,1,64]{0,2,1:T(8,128)(2,1)S(1)} %get-tuple-element.162), channel_id=1, source_target_pairs={{4,0},{8,4},{12,8},{5,1},{9,5},{13,9},{6,2},{10,6},{14,10},{7,3},{... | collective-permute-start | bytes 24584 | tf_op jit(solution)/shard_map/ppermute | solution.py:21
  121.3 5.9 %collective-permute-start.10 = (bf16[64,34,1]{0,2,1:T(2,128)(2,1)S(1)}, bf16[64,34,1]{0,2,1:T(2,128)(2,1)S(1)}, u32[]{:S(2)}, u32[]{:S(2)}) collective-permute-start(bf16[64,34,1]{0,2,1:T(2,128)(2,1)S(1)} %get-tuple-element.151), channel_id=1, source_target_pairs={{0,1},{1,2},{2,3},{4,5},{5,6},{6,7},{8,9},{9,10},{10,11},{12,13},{... | collective-permute-start | bytes 13064 | tf_op jit(solution)/shard_map/ppermute | solution.py:19
  124.6 5.1 %collective-permute-start.11 = (bf16[64,34,1]{0,2,1:T(2,128)(2,1)S(1)}, bf16[64,34,1]{0,2,1:T(2,128)(2,1)S(1)}, u32[]{:S(2)}, u32[]{:S(2)}) collective-permute-start(bf16[64,34,1]{0,2,1:T(2,128)(2,1)S(1)} %get-tuple-element.152), channel_id=1, source_target_pairs={{1,0},{2,1},{3,2},{5,4},{6,5},{7,6},{9,8},{10,9},{11,10},{13,12},{... | collective-permute-start | bytes 13064 | tf_op jit(solution)/shard_map/ppermute | solution.py:21
  132.2 3.2 %collective-permute-start.12 = (bf16[64,1,64]{0,2,1:T(8,128)(2,1)S(1)}, bf16[64,1,64]{0,2,1:T(8,128)(2,1)S(1)}, u32[]{:S(2)}, u32[]{:S(2)}) collective-permute-start(bf16[64,1,64]{0,2,1:T(8,128)(2,1)S(1)} %get-tuple-element.159), channel_id=1, source_target_pairs={{0,4},{4,8},{8,12},{1,5},{5,9},{9,13},{2,6},{6,10},{10,14},{3,7},{... | collective-permute-start | bytes 24584 | tf_op jit(solution)/shard_map/ppermute | solution.py:19
  133.8 4.5 %collective-permute-start.13 = (bf16[64,1,64]{0,2,1:T(8,128)(2,1)S(1)}, bf16[64,1,64]{0,2,1:T(8,128)(2,1)S(1)}, u32[]{:S(2)}, u32[]{:S(2)}) collective-permute-start(bf16[64,1,64]{0,2,1:T(8,128)(2,1)S(1)} %get-tuple-element.160), channel_id=1, source_target_pairs={{4,0},{8,4},{12,8},{5,1},{9,5},{13,9},{6,2},{10,6},{14,10},{7,3},{... | collective-permute-start | bytes 24584 | tf_op jit(solution)/shard_map/ppermute | solution.py:21
  138.4 5.9 %collective-permute-start.14 = (bf16[64,34,1]{0,2,1:T(2,128)(2,1)S(1)}, bf16[64,34,1]{0,2,1:T(2,128)(2,1)S(1)}, u32[]{:S(2)}, u32[]{:S(2)}) collective-permute-start(bf16[64,34,1]{0,2,1:T(2,128)(2,1)S(1)} %get-tuple-element.147), channel_id=1, source_target_pairs={{0,1},{1,2},{2,3},{4,5},{5,6},{6,7},{8,9},{9,10},{10,11},{12,13},{... | collective-permute-start | bytes 13064 | tf_op jit(solution)/shard_map/ppermute | solution.py:19
  141.7 5.1 %collective-permute-start.15 = (bf16[64,34,1]{0,2,1:T(2,128)(2,1)S(1)}, bf16[64,34,1]{0,2,1:T(2,128)(2,1)S(1)}, u32[]{:S(2)}, u32[]{:S(2)}) collective-permute-start(bf16[64,34,1]{0,2,1:T(2,128)(2,1)S(1)} %get-tuple-element.148), channel_id=1, source_target_pairs={{1,0},{2,1},{3,2},{5,4},{6,5},{7,6},{9,8},{10,9},{11,10},{13,12},{... | collective-permute-start | bytes 13064 | tf_op jit(solution)/shard_map/ppermute | solution.py:21
  149.2 3.5 %collective-permute-start.16 = (bf16[64,1,64]{0,2,1:T(8,128)(2,1)S(1)}, bf16[64,1,64]{0,2,1:T(8,128)(2,1)S(1)}, u32[]{:S(2)}, u32[]{:S(2)}) collective-permute-start(bf16[64,1,64]{0,2,1:T(8,128)(2,1)S(1)} %get-tuple-element.157), channel_id=1, source_target_pairs={{0,4},{4,8},{8,12},{1,5},{5,9},{9,13},{2,6},{6,10},{10,14},{3,7},{... | collective-permute-start | bytes 24584 | tf_op jit(solution)/shard_map/ppermute | solution.py:19
  150.8 4.5 %collective-permute-start.17 = (bf16[64,1,64]{0,2,1:T(8,128)(2,1)S(1)}, bf16[64,1,64]{0,2,1:T(8,128)(2,1)S(1)}, u32[]{:S(2)}, u32[]{:S(2)}) collective-permute-start(bf16[64,1,64]{0,2,1:T(8,128)(2,1)S(1)} %get-tuple-element.158), channel_id=1, source_target_pairs={{4,0},{8,4},{12,8},{5,1},{9,5},{13,9},{6,2},{10,6},{14,10},{7,3},{... | collective-permute-start | bytes 24584 | tf_op jit(solution)/shard_map/ppermute | solution.py:21
  155.4 6.3 %collective-permute-start.18 = (bf16[64,34,1]{0,2,1:T(2,128)(2,1)S(1)}, bf16[64,34,1]{0,2,1:T(2,128)(2,1)S(1)}, u32[]{:S(2)}, u32[]{:S(2)}) collective-permute-start(bf16[64,34,1]{0,2,1:T(2,128)(2,1)S(1)} %get-tuple-element.143), channel_id=1, source_target_pairs={{0,1},{1,2},{2,3},{4,5},{5,6},{6,7},{8,9},{9,10},{10,11},{12,13},{... | collective-permute-start | bytes 13064 | tf_op jit(solution)/shard_map/ppermute | solution.py:19
  158.7 5.1 %collective-permute-start.19 = (bf16[64,34,1]{0,2,1:T(2,128)(2,1)S(1)}, bf16[64,34,1]{0,2,1:T(2,128)(2,1)S(1)}, u32[]{:S(2)}, u32[]{:S(2)}) collective-permute-start(bf16[64,34,1]{0,2,1:T(2,128)(2,1)S(1)} %get-tuple-element.144), channel_id=1, source_target_pairs={{1,0},{2,1},{3,2},{5,4},{6,5},{7,6},{9,8},{10,9},{11,10},{13,12},{... | collective-permute-start | bytes 13064 | tf_op jit(solution)/shard_map/ppermute | solution.py:21
  (7 other events, 57.8 us)
where the time goes:
time: 170 us; the launch traced here: 168 us
  starting transfers between devices  59.8 us (35%)
  matrix products  52.6 us (31%)
  waiting for transfers between devices  44.1 us (26%)
  other arithmetic  6.97 us (4%)
  local copies, waits for them, and re-layouts  3.3 us (2%)
    ppermute x10, starting transfers between devices, with_halo(): lax.ppermute(tail, axis, [(i, (i + 1) % count) for i in range(ends)])  30.9 us
    ppermute x10, waiting for transfers between devices, with_halo(): lax.ppermute(head, axis, [((i + 1) % count, i) for i in range(ends)])  27.1 us
    dot_general x45, matrix products, conv_valid(): jnp.einsum('oc,crw->orw', weight[offset], window, preferred_element_type=...  16.7 us
    dot_general x8, matrix products, attend(): jnp.einsum('bhij,bjhd->bihd', probabilities, value_block, preferred_eleme...  16.1 us
    ppermute x10, starting transfers between devices, with_halo(): lax.ppermute(head, axis, [((i + 1) % count, i) for i in range(ends)])  16.1 us
    dot_general x8, matrix products, attend(): jnp.einsum('bhij,j->bhi', exponent, places, precision=lax.Precision.HIGHEST)  11.8 us
    all_to_all x1, waiting for transfers between devices, per_device(): lax.all_to_all(right_features, ('col', 'sub'), split_axis=0, concat_axis=...  7.79 us
    all_to_all x1, waiting for transfers between devices, per_device(): lax.all_to_all(left_features, ('col', 'sub'), split_axis=0, concat_axis=1...  6.1 us
  transfers between devices with their start and end apart: 23, of which 13 were waited for; matrix products, arithmetic and copies ran while one was open for 4% of the time, Pallas kernels for 0%

commit v1 on v0

--- a/solution.py
+++ b/solution.py
@@ -6,6 +6,18 @@
 C = 128
 HEADS = 8
 HEAD = 16
+
+
+def split_up(x, dim, length):
+    lengths = x.shape
+    blocks = x.reshape(*lengths[:dim], length, lengths[dim] // length, *lengths[dim + 1 :])
+    return jnp.moveaxis(blocks, dim, 0)
+
+
+def laid_out(tiles, dim):
+    tiles = jnp.moveaxis(tiles, 0, dim)
+    dims = tiles.shape
+    return tiles.reshape(*dims[:dim], dims[dim] * dims[dim + 1], *dims[dim + 2 :])
 
 
 def with_halo(cells, sides, width):
@@ -111,13 +123,18 @@
     head_out = blended.reshape(band_count, row_length, C)
     band_disparity = shift_sums.reshape(band_count, row_length) * (8.0 / (HEADS * row_length))
     band_occlusion = occlusion_logit(head_out, out_weight, occlusion_weight)
-    maps = lax.all_to_all(
-        jnp.stack([band_disparity, band_occlusion]),
-        ("col", "sub"),
-        split_axis=2,
-        concat_axis=1,
-        tiled=True,
-    )
+    shard = jnp.stack([band_disparity, band_occlusion])
+    size, index = (lax.axis_size(("col", "sub")), lax.axis_index(("col", "sub")))
+    tiles = split_up(shard, 2, size)
+    out = tiles
+    for step in range(1, size):
+        target, source_2 = ((index + step) % size, (index - step) % size)
+        sent = lax.dynamic_index_in_dim(tiles, target, 0)
+        other = lax.ppermute(
+            sent, ("col", "sub"), [(i_2, (i_2 + step) % size) for i_2 in range(size)]
+        )
+        out = lax.dynamic_update_slice_in_dim(out, other, source_2, axis=0)
+    maps = laid_out(out, 1)
     disparity = maps[0]
     occlusion = maps[1]
     stacked = jnp.concatenate([disparity[None], occlusion[None], left_image], axis=0).astype(

time: 170 us -> 152 us (0.89)
  matrix products: 52.6 us -> 39.1 us
  local copies, waits for them, and re-layouts: 3.3 us -> 1.36 us
  waiting for transfers between devices: 44.1 us -> 42.3 us
    dot_general x8, matrix products: 16.1 us -> 4.49 us  [attend(): jnp.einsum('bhij,bjhd->bihd', probabilities, value_block, preferred_eleme...]
    all_to_all x1 -> x0, starting transfers between devices: 4.1 us -> none  [per_device(): lax.all_to_all(jnp.stack([band_disparity, band_occlusion]), ('col', 'sub'...]
    all_to_all x1 -> x0, waiting for transfers between devices: 3.12 us -> none  [per_device(): lax.all_to_all(jnp.stack([band_disparity, band_occlusion]), ('col', 'sub'...]
    ppermute x0 -> x3, waiting for transfers between devices: none -> 2.92 us  [per_device(): lax.ppermute(sent, ('col', 'sub'), [(i_2, (i_2 + step) % size) for i_2 in...]
    ppermute x10, waiting for transfers between devices: 27.1 us -> 24.4 us  [with_halo(): lax.ppermute(head, axis, [((i + 1) % count, i) for i in range(ends)])]
    ppermute x10, starting transfers between devices: 30.9 us -> 33.2 us  [with_halo(): lax.ppermute(tail, axis, [(i, (i + 1) % count) for i in range(ends)])]
    ppermute x0 -> x3, starting transfers between devices: none -> 2.28 us  [per_device(): lax.ppermute(sent, ('col', 'sub'), [(i_2, (i_2 + step) % size) for i_2 in...]
  transfers between devices with their start and end apart: 23 -> 25, of which waited for: 13 -> 14; matrix products, arithmetic and copies ran while one was open for 4% -> 4% of each run, Pallas kernels for 0% -> 0%
where the time goes in v1:
time: 152 us; the launch traced here: 151 us
  starting transfers between devices  60.5 us (40%)
  waiting for transfers between devices  42.3 us (28%)
  matrix products  39.1 us (26%)
  other arithmetic  6.3 us (4%)
    ppermute x10, starting transfers between devices, with_halo(): lax.ppermute(tail, axis, [(i, (i + 1) % count) for i in range(ends)])  33.2 us
    ppermute x10, waiting for transfers between devices, with_halo(): lax.ppermute(head, axis, [((i + 1) % count, i) for i in range(ends)])  24.4 us
    dot_general x45, matrix products, conv_valid(): jnp.einsum('oc,crw->orw', weight[offset], window, preferred_element_type=...  16.7 us
    ppermute x10, starting transfers between devices, with_halo(): lax.ppermute(head, axis, [((i + 1) % count, i) for i in range(ends)])  16.2 us
    dot_general x8, matrix products, attend(): jnp.einsum('bhij,j->bhi', exponent, places, precision=lax.Precision.HIGHEST)  11.8 us
    all_to_all x1, waiting for transfers between devices, per_device(): lax.all_to_all(right_features, ('col', 'sub'), split_axis=0, concat_axis=...  7.79 us
    all_to_all x1, waiting for transfers between devices, per_device(): lax.all_to_all(left_features, ('col', 'sub'), split_axis=0, concat_axis=1...  6.88 us
    all_to_all x1, starting transfers between devices, per_device(): lax.all_to_all(left_features, ('col', 'sub'), split_axis=0, concat_axis=1...  4.49 us
  transfers between devices with their start and end apart: 25, of which 14 were waited for; matrix products, arithmetic and copies ran while one was open for 4% of the time, Pallas kernels for 0%

profile of v1, /device:TPU:1, one launch (start us, length us, event | category | flops | bytes accessed | tf_op | source)
XLA Modules:
  0.0 151.3 jit_solution(1694078275800073438)
XLA Ops:
  0.6 4.3 %all-to-all-start = ((bf16[32,64,128]{2,1,0:T(8,128)(2,1)}), bf16[32,64,128]{2,1,0:T(8,128)(2,1)S(1)}, u32[]{:S(2)}, u32[]{:S(2)}) async-start(bf16[32,64,128]{2,1,0:T(8,128)(2,1)} %param.13), calls=%async_computation | async-start | bytes 1048576 | tf_op jit(solution)/shard_map/all_to_all | solution.py:106
  4.9 7.8 %all-to-all-done = bf16[32,64,128]{2,1,0:T(8,128)(2,1)S(1)} async-done(((bf16[32,64,128]{2,1,0:T(8,128)(2,1)}), bf16[32,64,128]{2,1,0:T(8,128)(2,1)S(1)}, u32[]{:S(2)}, u32[]{:S(2)}) %all-to-all-start) | async-done | bytes 524320 | tf_op jit(solution)/shard_map/all_to_all | solution.py:106
  12.7 4.5 %all-to-all-start.1 = ((bf16[32,64,128]{2,1,0:T(8,128)(2,1)}), bf16[32,64,128]{2,1,0:T(8,128)(2,1)S(1)}, u32[]{:S(2)}, u32[]{:S(2)}) async-start(bf16[32,64,128]{2,1,0:T(8,128)(2,1)} %param.12), calls=%async_computation.1 | async-start | bytes 1048576 | tf_op jit(solution)/shard_map/all_to_all | solution.py:105
  18.3 6.9 %all-to-all-done.1 = bf16[32,64,128]{2,1,0:T(8,128)(2,1)S(1)} async-done(((bf16[32,64,128]{2,1,0:T(8,128)(2,1)}), bf16[32,64,128]{2,1,0:T(8,128)(2,1)S(1)}, u32[]{:S(2)}, u32[]{:S(2)}) %all-to-all-start.1) | async-done | bytes 524320 | tf_op jit(solution)/shard_map/all_to_all | solution.py:105
  25.6 24.2 %while.14 = (s32[]{:T(128)}, bf16[8,1,256,8,16]{2,4,3,1,0:T(8,128)(2,1)S(1)}, f32[8,1,256]{2,1,0:T(1,128)S(1)}, bf16[8,1,256,8,16]{2,4,3,1,0:T(8,128)(2,1)S(1)},...) while((s32[]{:T(128)}, ...), condition=%wide.region_4.5_spmd.clone.clone, body=%wide.region_0.4_spmd.clone.clone.sunk | while | flops 45713408 | bytes 9060433 | solution.py:119
  56.9 3.9 %collective-permute-start.3 = (bf16[5,1,64]{2,1,0:T(2,128)(2,1)S(1)}, bf16[5,1,64]{2,1,0:T(2,128)(2,1)S(1)}, u32[]{:S(2)}, u32[]{:S(2)}) collective-permute-start(bf16[5,1,64]{2,1,0:T(2,128)(2,1)S(1)} %get-tuple-element.153), channel_id=1, source_target_pairs={{0,4},{4,8},{8,12},{1,5},{5,9},{9,13},{2,6},{6,10},{10,14},{3,7},{... | collective-permute-start | bytes 1928 | tf_op jit(solution)/shard_map/ppermute | solution.py:31
  62.1 3.0 %collective-permute-done.4 = bf16[5,1,64]{2,1,0:T(2,128)(2,1)S(1)} collective-permute-done((bf16[5,1,64]{2,1,0:T(2,128)(2,1)S(1)}, bf16[5,1,64]{2,1,0:T(2,128)(2,1)S(1)}, u32[]{:S(2)}, u32[]{:S(2)}) %collective-permute-start.4) | collective-permute-done | bytes 672 | tf_op jit(solution)/shard_map/ppermute | solution.py:33
  65.2 3.4 %collective-permute-start.5 = (bf16[5,34,1]{2,1,0:T(8,128)(2,1)S(1)}, bf16[5,34,1]{2,1,0:T(8,128)(2,1)S(1)}, u32[]{:S(2)}, u32[]{:S(2)}) collective-permute-start(bf16[5,34,1]{2,1,0:T(8,128)(2,1)S(1)} %get-tuple-element.147), channel_id=1, source_target_pairs={{0,1},{1,2},{2,3},{4,5},{5,6},{6,7},{8,9},{9,10},{10,11},{12,13},{... | collective-permute-start | bytes 1028 | tf_op jit(solution)/shard_map/ppermute | solution.py:31
  71.0 3.1 %collective-permute-done.6 = bf16[5,34,1]{2,1,0:T(8,128)(2,1)S(1)} collective-permute-done((bf16[5,34,1]{2,1,0:T(8,128)(2,1)S(1)}, bf16[5,34,1]{2,1,0:T(8,128)(2,1)S(1)}, u32[]{:S(2)}, u32[]{:S(2)}) %collective-permute-start.6) | collective-permute-done | bytes 372 | tf_op jit(solution)/shard_map/ppermute | solution.py:33
  77.2 3.2 %collective-permute-start.7 = (bf16[64,1,64]{0,2,1:T(8,128)(2,1)S(1)}, bf16[64,1,64]{0,2,1:T(8,128)(2,1)S(1)}, u32[]{:S(2)}, u32[]{:S(2)}) collective-permute-start(bf16[64,1,64]{0,2,1:T(8,128)(2,1)S(1)} %get-tuple-element.139), channel_id=1, source_target_pairs={{0,4},{4,8},{8,12},{1,5},{5,9},{9,13},{2,6},{6,10},{10,14},{3,7},{... | collective-permute-start | bytes 24584 | tf_op jit(solution)/shard_map/ppermute | solution.py:31
  82.0 2.9 %collective-permute-done.8 = bf16[64,1,64]{0,2,1:T(8,128)(2,1)S(1)} collective-permute-done((bf16[64,1,64]{0,2,1:T(8,128)(2,1)S(1)}, bf16[64,1,64]{0,2,1:T(8,128)(2,1)S(1)}, u32[]{:S(2)}, u32[]{:S(2)}) %collective-permute-start.8) | collective-permute-done | bytes 8224 | tf_op jit(solution)/shard_map/ppermute | solution.py:33
  84.9 1.9 %collective-permute-start.10 = (bf16[64,34,1]{0,2,1:T(2,128)(2,1)S(1)}, bf16[64,34,1]{0,2,1:T(2,128)(2,1)S(1)}, u32[]{:S(2)}, u32[]{:S(2)}) collective-permute-start(bf16[64,34,1]{0,2,1:T(2,128)(2,1)S(1)} %get-tuple-element.132), channel_id=1, source_target_pairs={{1,0},{2,1},{3,2},{5,4},{6,5},{7,6},{9,8},{10,9},{11,10},{13,12},{... | collective-permute-start | bytes 13064 | tf_op jit(solution)/shard_map/ppermute | solution.py:33
  86.9 3.6 %collective-permute-start.9 = (bf16[64,34,1]{0,2,1:T(2,128)(2,1)S(1)}, bf16[64,34,1]{0,2,1:T(2,128)(2,1)S(1)}, u32[]{:S(2)}, u32[]{:S(2)}) collective-permute-start(bf16[64,34,1]{0,2,1:T(2,128)(2,1)S(1)} %get-tuple-element.131), channel_id=1, source_target_pairs={{0,1},{1,2},{2,3},{4,5},{5,6},{6,7},{8,9},{9,10},{10,11},{12,13},{... | collective-permute-start | bytes 13064 | tf_op jit(solution)/shard_map/ppermute | solution.py:31
  93.7 3.2 %collective-permute-start.11 = (bf16[64,1,64]{0,2,1:T(8,128)(2,1)S(1)}, bf16[64,1,64]{0,2,1:T(8,128)(2,1)S(1)}, u32[]{:S(2)}, u32[]{:S(2)}) collective-permute-start(bf16[64,1,64]{0,2,1:T(8,128)(2,1)S(1)} %get-tuple-element.137), channel_id=1, source_target_pairs={{0,4},{4,8},{8,12},{1,5},{5,9},{9,13},{2,6},{6,10},{10,14},{3,7},{... | collective-permute-start | bytes 24584 | tf_op jit(solution)/shard_map/ppermute | solution.py:31
  98.7 2.7 %collective-permute-done.12 = bf16[64,1,64]{0,2,1:T(8,128)(2,1)S(1)} collective-permute-done((bf16[64,1,64]{0,2,1:T(8,128)(2,1)S(1)}, bf16[64,1,64]{0,2,1:T(8,128)(2,1)S(1)}, u32[]{:S(2)}, u32[]{:S(2)}) %collective-permute-start.12) | collective-permute-done | bytes 8224 | tf_op jit(solution)/shard_map/ppermute | solution.py:33
  101.5 5.6 %collective-permute-start.13 = (bf16[64,34,1]{0,2,1:T(2,128)(2,1)S(1)}, bf16[64,34,1]{0,2,1:T(2,128)(2,1)S(1)}, u32[]{:S(2)}, u32[]{:S(2)}) collective-permute-start(bf16[64,34,1]{0,2,1:T(2,128)(2,1)S(1)} %get-tuple-element.127), channel_id=1, source_target_pairs={{0,1},{1,2},{2,3},{4,5},{5,6},{6,7},{8,9},{9,10},{10,11},{12,13},{... | collective-permute-start | bytes 13064 | tf_op jit(solution)/shard_map/ppermute | solution.py:31
  109.7 2.5 %collective-permute-done.14 = bf16[64,34,1]{0,2,1:T(2,128)(2,1)S(1)} collective-permute-done((bf16[64,34,1]{0,2,1:T(2,128)(2,1)S(1)}, bf16[64,34,1]{0,2,1:T(2,128)(2,1)S(1)}, u32[]{:S(2)}, u32[]{:S(2)}) %collective-permute-start.14) | collective-permute-done | bytes 4384 | tf_op jit(solution)/shard_map/ppermute | solution.py:33
  114.7 1.9 %collective-permute-start.15 = (bf16[64,1,64]{0,2,1:T(8,128)(2,1)S(1)}, bf16[64,1,64]{0,2,1:T(8,128)(2,1)S(1)}, u32[]{:S(2)}, u32[]{:S(2)}) collective-permute-start(bf16[64,1,64]{0,2,1:T(8,128)(2,1)S(1)} %get-tuple-element.135), channel_id=1, source_target_pairs={{0,4},{4,8},{8,12},{1,5},{5,9},{9,13},{2,6},{6,10},{10,14},{3,7},{... | collective-permute-start | bytes 24584 | tf_op jit(solution)/shard_map/ppermute | solution.py:31
  118.2 2.9 %collective-permute-done.16 = bf16[64,1,64]{0,2,1:T(8,128)(2,1)S(1)} collective-permute-done((bf16[64,1,64]{0,2,1:T(8,128)(2,1)S(1)}, bf16[64,1,64]{0,2,1:T(8,128)(2,1)S(1)}, u32[]{:S(2)}, u32[]{:S(2)}) %collective-permute-start.16) | collective-permute-done | bytes 8224 | tf_op jit(solution)/shard_map/ppermute | solution.py:33
  121.1 3.4 %collective-permute-start.17 = (bf16[64,34,1]{0,2,1:T(2,128)(2,1)S(1)}, bf16[64,34,1]{0,2,1:T(2,128)(2,1)S(1)}, u32[]{:S(2)}, u32[]{:S(2)}) collective-permute-start(bf16[64,34,1]{0,2,1:T(2,128)(2,1)S(1)} %get-tuple-element.123), channel_id=1, source_target_pairs={{0,1},{1,2},{2,3},{4,5},{5,6},{6,7},{8,9},{9,10},{10,11},{12,13},{... | collective-permute-start | bytes 13064 | tf_op jit(solution)/shard_map/ppermute | solution.py:31
  127.0 2.5 %collective-permute-done.18 = bf16[64,34,1]{0,2,1:T(2,128)(2,1)S(1)} collective-permute-done((bf16[64,34,1]{0,2,1:T(2,128)(2,1)S(1)}, bf16[64,34,1]{0,2,1:T(2,128)(2,1)S(1)}, u32[]{:S(2)}, u32[]{:S(2)}) %collective-permute-start.18) | collective-permute-done | bytes 4384 | tf_op jit(solution)/shard_map/ppermute | solution.py:33
  135.4 2.7 %collective-permute-done.20 = bf16[64,1,64]{0,2,1:T(8,128)(2,1)S(1)} collective-permute-done((bf16[64,1,64]{0,2,1:T(8,128)(2,1)S(1)}, bf16[64,1,64]{0,2,1:T(8,128)(2,1)S(1)}, u32[]{:S(2)}, u32[]{:S(2)}) %collective-permute-start.20) | collective-permute-done | bytes 8224 | tf_op jit(solution)/shard_map/ppermute | solution.py:33
  138.1 3.4 %collective-permute-start.21 = (bf16[64,34,1]{0,2,1:T(2,128)(2,1)S(1)}, bf16[64,34,1]{0,2,1:T(2,128)(2,1)S(1)}, u32[]{:S(2)}, u32[]{:S(2)}) collective-permute-start(bf16[64,34,1]{0,2,1:T(2,128)(2,1)S(1)} %get-tuple-element.119), channel_id=1, source_target_pairs={{0,1},{1,2},{2,3},{4,5},{5,6},{6,7},{8,9},{9,10},{10,11},{12,13},{... | collective-permute-start | bytes 13064 | tf_op jit(solution)/shard_map/ppermute | solution.py:31
  144.5 2.1 %collective-permute-done.22 = bf16[64,34,1]{0,2,1:T(2,128)(2,1)S(1)} collective-permute-done((bf16[64,34,1]{0,2,1:T(2,128)(2,1)S(1)}, bf16[64,34,1]{0,2,1:T(2,128)(2,1)S(1)}, u32[]{:S(2)}, u32[]{:S(2)}) %collective-permute-start.22) | collective-permute-done | bytes 4384 | tf_op jit(solution)/shard_map/ppermute | solution.py:33
  (201 shorter events, 68.2 us)
Async XLA Ops:
  0.6 12.1 %all-to-all-start = ((bf16[32,64,128]{2,1,0:T(8,128)(2,1)}), bf16[32,64,128]{2,1,0:T(8,128)(2,1)S(1)}, u32[]{:S(2)}, u32[]{:S(2)}) async-start(bf16[32,64,128]{2,1,0:T(8,128)(2,1)} %param.13), calls=%async_computation | async-start | bytes 1048576 | tf_op jit(solution)/shard_map/all_to_all | solution.py:106
  12.7 12.5 %all-to-all-start.1 = ((bf16[32,64,128]{2,1,0:T(8,128)(2,1)}), bf16[32,64,128]{2,1,0:T(8,128)(2,1)S(1)}, u32[]{:S(2)}, u32[]{:S(2)}) async-start(bf16[32,64,128]{2,1,0:T(8,128)(2,1)} %param.12), calls=%async_computation.1 | async-start | bytes 1048576 | tf_op jit(solution)/shard_map/all_to_all | solution.py:105
  52.3 2.7 %collective-permute-start.1 = (f32[1,2,8,64]{3,0,2,1:T(1,128)S(1)}, f32[1,2,8,64]{3,0,2,1:T(1,128)S(1)}, u32[]{:S(2)}, u32[]{:S(2)}) collective-permute-start(f32[1,2,8,64]{3,0,2,1:T(1,128)S(1)} %get-tuple-element.162), channel_id=1, source_target_pairs={{0,2},{1,3},{2,0},{3,1},{4,6},{5,7},{6,4},{7,5},{8,10},{9,11},{10,... | collective-permute-start | bytes 12296 | tf_op jit(solution)/shard_map/ppermute | solution.py:133
  53.7 3.1 %collective-permute-start.2 = (f32[1,2,8,64]{3,0,2,1:T(1,128)S(1)}, f32[1,2,8,64]{3,0,2,1:T(1,128)S(1)}, u32[]{:S(2)}, u32[]{:S(2)}) collective-permute-start(f32[1,2,8,64]{3,0,2,1:T(1,128)S(1)} %get-tuple-element.161), channel_id=1, source_target_pairs={{0,3},{1,0},{2,1},{3,2},{4,7},{5,4},{6,5},{7,6},{8,11},{9,8},{10,9... | collective-permute-start | bytes 12296 | tf_op jit(solution)/shard_map/ppermute | solution.py:133
  56.9 5.2 %collective-permute-start.3 = (bf16[5,1,64]{2,1,0:T(2,128)(2,1)S(1)}, bf16[5,1,64]{2,1,0:T(2,128)(2,1)S(1)}, u32[]{:S(2)}, u32[]{:S(2)}) collective-permute-start(bf16[5,1,64]{2,1,0:T(2,128)(2,1)S(1)} %get-tuple-element.153), channel_id=1, source_target_pairs={{0,4},{4,8},{8,12},{1,5},{5,9},{9,13},{2,6},{6,10},{10,14},{3,7},{... | collective-permute-start | bytes 1928 | tf_op jit(solution)/shard_map/ppermute | solution.py:31
  60.8 4.3 %collective-permute-start.4 = (bf16[5,1,64]{2,1,0:T(2,128)(2,1)S(1)}, bf16[5,1,64]{2,1,0:T(2,128)(2,1)S(1)}, u32[]{:S(2)}, u32[]{:S(2)}) collective-permute-start(bf16[5,1,64]{2,1,0:T(2,128)(2,1)S(1)} %get-tuple-element.154), channel_id=1, source_target_pairs={{4,0},{8,4},{12,8},{5,1},{9,5},{13,9},{6,2},{10,6},{14,10},{7,3},{... | collective-permute-start | bytes 1928 | tf_op jit(solution)/shard_map/ppermute | solution.py:33
  65.2 5.7 %collective-permute-start.5 = (bf16[5,34,1]{2,1,0:T(8,128)(2,1)S(1)}, bf16[5,34,1]{2,1,0:T(8,128)(2,1)S(1)}, u32[]{:S(2)}, u32[]{:S(2)}) collective-permute-start(bf16[5,34,1]{2,1,0:T(8,128)(2,1)S(1)} %get-tuple-element.147), channel_id=1, source_target_pairs={{0,1},{1,2},{2,3},{4,5},{5,6},{6,7},{8,9},{9,10},{10,11},{12,13},{... | collective-permute-start | bytes 1028 | tf_op jit(solution)/shard_map/ppermute | solution.py:31
  68.6 5.4 %collective-permute-start.6 = (bf16[5,34,1]{2,1,0:T(8,128)(2,1)S(1)}, bf16[5,34,1]{2,1,0:T(8,128)(2,1)S(1)}, u32[]{:S(2)}, u32[]{:S(2)}) collective-permute-start(bf16[5,34,1]{2,1,0:T(8,128)(2,1)S(1)} %get-tuple-element.148), channel_id=1, source_target_pairs={{1,0},{2,1},{3,2},{5,4},{6,5},{7,6},{9,8},{10,9},{11,10},{13,12},{... | collective-permute-start | bytes 1028 | tf_op jit(solution)/shard_map/ppermute | solution.py:33
  77.2 4.8 %collective-permute-start.7 = (bf16[64,1,64]{0,2,1:T(8,128)(2,1)S(1)}, bf16[64,1,64]{0,2,1:T(8,128)(2,1)S(1)}, u32[]{:S(2)}, u32[]{:S(2)}) collective-permute-start(bf16[64,1,64]{0,2,1:T(8,128)(2,1)S(1)} %get-tuple-element.139), channel_id=1, source_target_pairs={{0,4},{4,8},{8,12},{1,5},{5,9},{9,13},{2,6},{6,10},{10,14},{3,7},{... | collective-permute-start | bytes 24584 | tf_op jit(solution)/shard_map/ppermute | solution.py:31
  80.4 4.5 %collective-permute-start.8 = (bf16[64,1,64]{0,2,1:T(8,128)(2,1)S(1)}, bf16[64,1,64]{0,2,1:T(8,128)(2,1)S(1)}, u32[]{:S(2)}, u32[]{:S(2)}) collective-permute-start(bf16[64,1,64]{0,2,1:T(8,128)(2,1)S(1)} %get-tuple-element.140), channel_id=1, source_target_pairs={{4,0},{8,4},{12,8},{5,1},{9,5},{13,9},{6,2},{10,6},{14,10},{7,3},{... | collective-permute-start | bytes 24584 | tf_op jit(solution)/shard_map/ppermute | solution.py:33
  84.9 6.2 %collective-permute-start.10 = (bf16[64,34,1]{0,2,1:T(2,128)(2,1)S(1)}, bf16[64,34,1]{0,2,1:T(2,128)(2,1)S(1)}, u32[]{:S(2)}, u32[]{:S(2)}) collective-permute-start(bf16[64,34,1]{0,2,1:T(2,128)(2,1)S(1)} %get-tuple-element.132), channel_id=1, source_target_pairs={{1,0},{2,1},{3,2},{5,4},{6,5},{7,6},{9,8},{10,9},{11,10},{13,12},{... | collective-permute-start | bytes 13064 | tf_op jit(solution)/shard_map/ppermute | solution.py:33
  86.9 4.5 %collective-permute-start.9 = (bf16[64,34,1]{0,2,1:T(2,128)(2,1)S(1)}, bf16[64,34,1]{0,2,1:T(2,128)(2,1)S(1)}, u32[]{:S(2)}, u32[]{:S(2)}) collective-permute-start(bf16[64,34,1]{0,2,1:T(2,128)(2,1)S(1)} %get-tuple-element.131), channel_id=1, source_target_pairs={{0,1},{1,2},{2,3},{4,5},{5,6},{6,7},{8,9},{9,10},{10,11},{12,13},{... | collective-permute-start | bytes 13064 | tf_op jit(solution)/shard_map/ppermute | solution.py:31
  93.7 5.0 %collective-permute-start.11 = (bf16[64,1,64]{0,2,1:T(8,128)(2,1)S(1)}, bf16[64,1,64]{0,2,1:T(8,128)(2,1)S(1)}, u32[]{:S(2)}, u32[]{:S(2)}) collective-permute-start(bf16[64,1,64]{0,2,1:T(8,128)(2,1)S(1)} %get-tuple-element.137), channel_id=1, source_target_pairs={{0,4},{4,8},{8,12},{1,5},{5,9},{9,13},{2,6},{6,10},{10,14},{3,7},{... | collective-permute-start | bytes 24584 | tf_op jit(solution)/shard_map/ppermute | solution.py:31
  97.0 4.5 %collective-permute-start.12 = (bf16[64,1,64]{0,2,1:T(8,128)(2,1)S(1)}, bf16[64,1,64]{0,2,1:T(8,128)(2,1)S(1)}, u32[]{:S(2)}, u32[]{:S(2)}) collective-permute-start(bf16[64,1,64]{0,2,1:T(8,128)(2,1)S(1)} %get-tuple-element.138), channel_id=1, source_target_pairs={{4,0},{8,4},{12,8},{5,1},{9,5},{13,9},{6,2},{10,6},{14,10},{7,3},{... | collective-permute-start | bytes 24584 | tf_op jit(solution)/shard_map/ppermute | solution.py:33
  101.5 8.2 %collective-permute-start.13 = (bf16[64,34,1]{0,2,1:T(2,128)(2,1)S(1)}, bf16[64,34,1]{0,2,1:T(2,128)(2,1)S(1)}, u32[]{:S(2)}, u32[]{:S(2)}) collective-permute-start(bf16[64,34,1]{0,2,1:T(2,128)(2,1)S(1)} %get-tuple-element.127), channel_id=1, source_target_pairs={{0,1},{1,2},{2,3},{4,5},{5,6},{6,7},{8,9},{9,10},{10,11},{12,13},{... | collective-permute-start | bytes 13064 | tf_op jit(solution)/shard_map/ppermute | solution.py:31
  107.1 5.1 %collective-permute-start.14 = (bf16[64,34,1]{0,2,1:T(2,128)(2,1)S(1)}, bf16[64,34,1]{0,2,1:T(2,128)(2,1)S(1)}, u32[]{:S(2)}, u32[]{:S(2)}) collective-permute-start(bf16[64,34,1]{0,2,1:T(2,128)(2,1)S(1)} %get-tuple-element.128), channel_id=1, source_target_pairs={{1,0},{2,1},{3,2},{5,4},{6,5},{7,6},{9,8},{10,9},{11,10},{13,12},{... | collective-permute-start | bytes 13064 | tf_op jit(solution)/shard_map/ppermute | solution.py:33
  114.7 3.5 %collective-permute-start.15 = (bf16[64,1,64]{0,2,1:T(8,128)(2,1)S(1)}, bf16[64,1,64]{0,2,1:T(8,128)(2,1)S(1)}, u32[]{:S(2)}, u32[]{:S(2)}) collective-permute-start(bf16[64,1,64]{0,2,1:T(8,128)(2,1)S(1)} %get-tuple-element.135), channel_id=1, source_target_pairs={{0,4},{4,8},{8,12},{1,5},{5,9},{9,13},{2,6},{6,10},{10,14},{3,7},{... | collective-permute-start | bytes 24584 | tf_op jit(solution)/shard_map/ppermute | solution.py:31
  116.6 4.5 %collective-permute-start.16 = (bf16[64,1,64]{0,2,1:T(8,128)(2,1)S(1)}, bf16[64,1,64]{0,2,1:T(8,128)(2,1)S(1)}, u32[]{:S(2)}, u32[]{:S(2)}) collective-permute-start(bf16[64,1,64]{0,2,1:T(8,128)(2,1)S(1)} %get-tuple-element.136), channel_id=1, source_target_pairs={{4,0},{8,4},{12,8},{5,1},{9,5},{13,9},{6,2},{10,6},{14,10},{7,3},{... | collective-permute-start | bytes 24584 | tf_op jit(solution)/shard_map/ppermute | solution.py:33
  121.1 5.9 %collective-permute-start.17 = (bf16[64,34,1]{0,2,1:T(2,128)(2,1)S(1)}, bf16[64,34,1]{0,2,1:T(2,128)(2,1)S(1)}, u32[]{:S(2)}, u32[]{:S(2)}) collective-permute-start(bf16[64,34,1]{0,2,1:T(2,128)(2,1)S(1)} %get-tuple-element.123), channel_id=1, source_target_pairs={{0,1},{1,2},{2,3},{4,5},{5,6},{6,7},{8,9},{9,10},{10,11},{12,13},{... | collective-permute-start | bytes 13064 | tf_op jit(solution)/shard_map/ppermute | solution.py:31
  124.5 5.1 %collective-permute-start.18 = (bf16[64,34,1]{0,2,1:T(2,128)(2,1)S(1)}, bf16[64,34,1]{0,2,1:T(2,128)(2,1)S(1)}, u32[]{:S(2)}, u32[]{:S(2)}) collective-permute-start(bf16[64,34,1]{0,2,1:T(2,128)(2,1)S(1)} %get-tuple-element.124), channel_id=1, source_target_pairs={{1,0},{2,1},{3,2},{5,4},{6,5},{7,6},{9,8},{10,9},{11,10},{13,12},{... | collective-permute-start | bytes 13064 | tf_op jit(solution)/shard_map/ppermute | solution.py:33
  132.0 3.5 %collective-permute-start.19 = (bf16[64,1,64]{0,2,1:T(8,128)(2,1)S(1)}, bf16[64,1,64]{0,2,1:T(8,128)(2,1)S(1)}, u32[]{:S(2)}, u32[]{:S(2)}) collective-permute-start(bf16[64,1,64]{0,2,1:T(8,128)(2,1)S(1)} %get-tuple-element.133), channel_id=1, source_target_pairs={{0,4},{4,8},{8,12},{1,5},{5,9},{9,13},{2,6},{6,10},{10,14},{3,7},{... | collective-permute-start | bytes 24584 | tf_op jit(solution)/shard_map/ppermute | solution.py:31
  133.6 4.5 %collective-permute-start.20 = (bf16[64,1,64]{0,2,1:T(8,128)(2,1)S(1)}, bf16[64,1,64]{0,2,1:T(8,128)(2,1)S(1)}, u32[]{:S(2)}, u32[]{:S(2)}) collective-permute-start(bf16[64,1,64]{0,2,1:T(8,128)(2,1)S(1)} %get-tuple-element.134), channel_id=1, source_target_pairs={{4,0},{8,4},{12,8},{5,1},{9,5},{13,9},{6,2},{10,6},{14,10},{7,3},{... | collective-permute-start | bytes 24584 | tf_op jit(solution)/shard_map/ppermute | solution.py:33
  138.1 6.3 %collective-permute-start.21 = (bf16[64,34,1]{0,2,1:T(2,128)(2,1)S(1)}, bf16[64,34,1]{0,2,1:T(2,128)(2,1)S(1)}, u32[]{:S(2)}, u32[]{:S(2)}) collective-permute-start(bf16[64,34,1]{0,2,1:T(2,128)(2,1)S(1)} %get-tuple-element.119), channel_id=1, source_target_pairs={{0,1},{1,2},{2,3},{4,5},{5,6},{6,7},{8,9},{9,10},{10,11},{12,13},{... | collective-permute-start | bytes 13064 | tf_op jit(solution)/shard_map/ppermute | solution.py:31
  141.5 5.1 %collective-permute-start.22 = (bf16[64,34,1]{0,2,1:T(2,128)(2,1)S(1)}, bf16[64,34,1]{0,2,1:T(2,128)(2,1)S(1)}, u32[]{:S(2)}, u32[]{:S(2)}) collective-permute-start(bf16[64,34,1]{0,2,1:T(2,128)(2,1)S(1)} %get-tuple-element.120), channel_id=1, source_target_pairs={{1,0},{2,1},{3,2},{5,4},{6,5},{7,6},{9,8},{10,9},{11,10},{13,12},{... | collective-permute-start | bytes 13064 | tf_op jit(solution)/shard_map/ppermute | solution.py:33
  (9 other events, 76.8 us)
